TPU v7x, 32 devices: a whole 2x2x4 slice. The times are simulated.
32 devices in a mesh: tm: 8 (over z, x), feat: 4 (over y, core).
Axes of the slice: x: 2, y: 2, z: 4, core: 2. Of those that a mesh axis runs over, the one named last changes fastest.
Arguments:
- coords: float32 [512, 3, 8, 256], P('tm'), may hold values from -12 to 12, as said below
- set_a: int32 [128], replicated, may hold values from 0 to 255
- set_b: int32 [128], replicated, may hold values from 0 to 255
Outputs:
- c00: float32 [16384, 16384], P('feat', 'tm')
- c0t: float32 [16384, 16384], P('feat', 'tm')
Inputs may be any that keep to these rules, and one draw needn't show every extreme that they name: `coords`: positions of a folding protein.
All inputs are finite; a program needn't handle non-finite values.
Results may differ from a plain program's by a relative error of at most 0.0003.
Values may be sent and summed in bfloat16 or wider, within the bound.
A program may use at most 128 MiB of HBM per device.

v0:
```python
import jax
import jax.numpy as jnp
from jax import lax
from jax.sharding import PartitionSpec as P

LAG = 64


contact_radius = 1.2
contact_width = 0.25


def contact_features(positions, index_a, index_b):
    part_a = jnp.take(positions, index_a, axis=3)
    part_b = jnp.take(positions, index_b, axis=3)
    frame_rows = positions.shape[0]
    summed = jnp.zeros((frame_rows, part_a.shape[3], part_b.shape[3]), jnp.float32)
    for first_atom in range(part_a.shape[2]):
        square = jnp.zeros(
            (frame_rows, part_b.shape[2], part_a.shape[3], part_b.shape[3]), jnp.float32
        )
        for component in range(3):
            difference = (
                part_a[:, component, first_atom, :][:, None, :, None]
                - part_b[:, component, :, :][:, :, None, :]
            )
            square = square + difference * difference
        summed = summed + jnp.sum(
            jax.nn.sigmoid((contact_radius - jnp.sqrt(square)) / contact_width), axis=1
        )
    summed = summed / float(part_a.shape[2])
    return summed.reshape(frame_rows, part_a.shape[3] * part_b.shape[3])


def contract_frames(left, right):
    return lax.dot_general(
        left, right, (((0,), (0,)), ((), ())), preferred_element_type=jnp.float32
    )


def pair_sums(frames_block, pairs):
    early = frames_block[:pairs].astype(jnp.float32)
    later = frames_block[LAG:].astype(jnp.float32)
    padding = jnp.zeros((LAG, frames_block.shape[1]), jnp.bfloat16)
    plus = jnp.concatenate([(early + later).astype(jnp.bfloat16), padding], axis=0)
    minus = jnp.concatenate([(early - later).astype(jnp.bfloat16), padding], axis=0)
    return (plus, minus)


def per_device(coords, set_a, set_b):
    feat_count = lax.axis_size("feat")
    feat_index = lax.axis_index("feat")
    rows_a = set_a.shape[0] // feat_count
    index_a = lax.dynamic_slice_in_dim(set_a, feat_index * rows_a, rows_a)
    lifted = contact_features(coords, index_a, set_b)
    frame_rows = coords.shape[0]
    time_count = lax.axis_size("tm")
    time_index = lax.axis_index("tm")
    frames_all = frame_rows * time_count
    pairs = frames_all - LAG
    frame_ids = time_index * frame_rows + jnp.arange(frame_rows, dtype=jnp.int32)
    weight = (frame_ids < pairs).astype(jnp.float32) + (frame_ids >= LAG).astype(jnp.float32)
    local_sums = jnp.dot(weight, lifted, precision=lax.Precision.HIGHEST)
    means = lax.psum(local_sums, "tm") / (2.0 * pairs)
    centered = (lifted - means[None, :]).astype(jnp.bfloat16)
    centered = lax.optimization_barrier(centered)
    every_feature = lax.all_gather(centered, "feat", axis=1, tiled=True)
    column_block = lax.all_to_all(every_feature, "tm", split_axis=1, concat_axis=0, tiled=True)
    plus_cols, minus_cols = pair_sums(column_block, pairs)
    gathered = lax.all_gather(centered, "tm", axis=0, tiled=True)
    plus_rows, minus_rows = pair_sums(gathered, pairs)
    sum_plus = contract_frames(plus_rows, plus_cols)
    sum_minus = contract_frames(minus_rows, minus_cols)
    c00 = (sum_plus + sum_minus) / (4.0 * pairs)
    c0t = (sum_plus - sum_minus) / (4.0 * pairs)
    return (c00, c0t)


def solution(mesh):
    placed = (P("tm", None, None, None), P(), P())
    return jax.shard_map(
        per_device,
        mesh=mesh,
        in_specs=placed,
        out_specs=(P("feat", "tm"), P("feat", "tm")),
        check_vma=False,
    )
```

profile of v0, /device:TPU:7, one launch (start us, length us, event | category | flops | bytes accessed | tf_op | source)
XLA Modules:
  0.0 300.7 jit_solution(4928474648640069345)
XLA Ops:
  7.2 0.7 compare_and_fusion
  7.9 0.7 compare_select_fusion
  8.5 0.7 compare_and_fusion.1
  9.3 2.3 copy.95
  11.6 0.6 gather_fusion
  12.3 0.3 fusion.34
  12.7 1.9 gather_fusion.1
  14.6 1.6 select_bitcast_fusion
  18.6 0.2 copy.102
  19.0 19.8 %fusion.7 = (f32[64,32,128]{2,1,0:T(8,128)S(1)}, f32[64,32,128]{2,1,0:T(8,128)S(1)}, f32[64,32,128]{2,1,0:T(8,128)S(1)}) fusion(f32[64,8,128]{2,1,0:T(8,128)S(1)} %copy.102, f32[64,32]{1,0:T(8,128)S(1)} %copy.101, f32[64,8,128]{2,1,0:T(8,128)S(1)} %copy.100, f32[64,32]{1,0:T(8,128)S(1)} %copy.99, f32[64,8,128]{2,1,0:T(8,128)S(1)} %copy.98, ...), kind=kLoop, calls=%fused_computation.21 | loop fusion | flops 87293952 | bytes 4005888 | tf_op jit(solution)/shard_map/reduce_sum | solution.py:28
  38.8 31.7 %fusion.6 = (f32[64,32,128]{2,1,0:T(8,128)S(1)}, f32[64,32,128]{2,1,0:T(8,128)S(1)}, f32[64,32,128]{2,1,0:T(8,128)S(1)}, f32[64,32,128]{2,1,0:T(8,128)S(1)}, f32[64,32,128]{2,1,0:T(8,128)S(1)}) fusion(f32[64,32]{1,0:T(8,128)S(1)} %copy.105, f32[64,32]{1,0:T(8,128)S(1)} %copy.104, f32[64,32]{1,0:T(8,128)S(1)} %copy.103, f32[64,8,128]{2,1,0:T(8,128)S(1)} %copy.102, ...), kind=kLoop, calls=%fused_computation.19 | loop fusion | flops 145489920 | bytes 6152192 | tf_op jit(solution)/shard_map/reduce_sum | solution.py:28
  70.5 1.0 add_multiply_fusion.1
  71.6 1.2 fusion.18
  72.7 26.1 %psum.7 = f32[4096]{0:T(1024)S(1)} all-reduce(f32[4096]{0:T(1024)S(1)} %bitcast.59), channel_id=1, replica_groups=mesh['tm'=8,'feat'=4] {'tm'}, use_global_device_ids=true, to_apply=%region_8.9 | all-reduce | flops 4096 | bytes 32768 | tf_op jit(solution)/shard_map/psum | solution.py:64
  98.8 1.4 fusion.20
  100.3 0.7 all-gather.3.cloned.1.call-update
  101.0 29.9 %all-gather.5.cloned.1.call-done = bf16[64,16384]{1,0:T(8,128)(2,1)} async-done(((bf16[64,4096]{1,0:T(8,128)(2,1)}), bf16[64,16384]{1,0:T(8,128)(2,1)}) %all-gather.5.cloned.1.call-update) | async-done | bytes 2097168 | tf_op jit(solution)/shard_map/all_gather | solution.py:67
  130.9 1.7 copy.133
  132.7 86.8 %all_to_all.16 = bf16[64,8,2048]{2,0,1:T(8,128)(2,1)S(1)} all-to-all(bf16[64,8,2048]{2,0,1:T(8,128)(2,1)S(1)} %bitcast.55), channel_id=1, replica_groups=mesh['tm'=8,'feat'=4] {'tm'}, dimensions={1} | all-to-all | bytes 4194304 | tf_op jit(solution)/shard_map/all_to_all | solution.py:68
  219.5 2.1 fusion.15
  221.6 15.7 %all-gather.3.cloned.1.call-done = bf16[512,4096]{1,0:T(8,128)(2,1)} async-done(((bf16[64,4096]{1,0:T(8,128)(2,1)}), bf16[512,4096]{1,0:T(8,128)(2,1)}) %all-gather.3.cloned.1.call-update) | async-done | bytes 4194320 | tf_op jit(solution)/shard_map/all_gather | solution.py:70
  237.3 5.5 %fusion.9 = (bf16[448,4096]{1,0:T(8,128)(2,1)S(1)}, bf16[448,4096]{1,0:T(8,128)(2,1)}) fusion(bf16[512,4096]{1,0:T(8,128)(2,1)} %all-gather.3.cloned.1.call-done), kind=kLoop, calls=%fused_computation.23 | loop fusion | flops 11010048 | bytes 14680064 | tf_op jit(solution)/shard_map/convert_element_type | solution.py:46
  242.9 16.3 %fusion.10 = f32[4096,2048]{1,0:T(8,128)} fusion(bf16[448,4096]{1,0:T(8,128)(2,1)S(1)} %get-tuple-element.14, bf16[448,2048]{1,0:T(8,128)(2,1)S(1)} %bitcast.58), kind=kOutput, calls=%fused_computation.26 | convolution fusion | flops 8589934592 | bytes 39059456 | tf_op jit(solution)/shard_map/dot_general | solution.py:36
  259.1 34.7 %subtract_multiply_fusion = (f32[4096,2048]{1,0:T(8,128)}, f32[4096,2048]{1,0:T(8,128)}) fusion(f32[4096,2048]{1,0:T(8,128)} %fusion.10, bf16[448,2048]{1,0:T(8,128)(2,1)S(1)} %bitcast.56, bf16[448,4096]{1,0:T(8,128)(2,1)} %get-tuple-element.15), kind=kOutput, calls=%fused_computation.2 | convolution fusion | flops 8623489024 | bytes 106168320 | tf_op jit(solution)/shard_map/dot_general | solution.py:36
  (37 shorter events, 2.8 us)
Async XLA Ops:
  7.2 123.8 %all-gather.5.cloned.1.call-start = ((), (), s32[]{:S(2)}) async-start(), calls=%async_computation.2 | async-start | bytes 2621440 | tf_op jit(solution)/shard_map/all_gather | solution.py:67
  100.2 137.1 %all-gather.3.cloned.1.call-start = ((), (), s32[]{:S(2)}) async-start(), calls=%async_computation.1 | async-start | bytes 4718592 | tf_op jit(solution)/shard_map/all_gather | solution.py:70
  237.3 5.5 %copy-start = (bf16[7,64,2048]{2,1,0:T(8,128)(2,1)S(1)}, bf16[7,64,2048]{2,1,0:T(8,128)(2,1)}, u32[]{:S(2)}) copy-start(bf16[7,64,2048]{2,1,0:T(8,128)(2,1)} %get-tuple-element.16) | copy-start | bytes 5505028
Sparse Core Ops, SparseCore 0:
  100.4 30.5 all-gather.4
  133.6 103.6 all-gather.2
where the time goes:
time: 303 us; the launch traced here: 301 us
  blocking collectives  113 us (37%)
  other arithmetic  65.3 us (22%)
  matrix products  52.1 us (17%)
  waiting for transfers between devices  46.4 us (15%)
  between operations  14.2 us (5%)
  local copies, waits for them, and re-layouts  9.68 us (3%)
    all_to_all x1, blocking collectives, per_device(): lax.all_to_all(every_feature, 'tm', split_axis=1, concat_axis=0, tiled=True)  86.8 us
    reduce_sum x2, other arithmetic, contact_features(): jnp.sum(jax.nn.sigmoid((contact_radius - jnp.sqrt(square)) / contact_widt...  51.5 us
    dot_general x2, matrix products, contract_frames(): lax.dot_general(left, right, (((0,), (0,)), ((), ())), preferred_element_...  51 us
    all_gather x1, waiting for transfers between devices, per_device(): every_feature = lax.all_gather(centered, 'feat', axis=1, tiled=True)  29.9 us
    psum x1, blocking collectives, per_device(): means = lax.psum(local_sums, 'tm') / (2.0 * pairs)  26.1 us
    all_gather x1, waiting for transfers between devices, per_device(): gathered = lax.all_gather(centered, 'tm', axis=0, tiled=True)  15.7 us
    convert_element_type x2, other arithmetic, pair_sums(): (early - later).astype(jnp.bfloat16)  7.62 us
  transfers between devices with their start and end apart: 2, of which 2 were waited for; matrix products, arithmetic and copies ran while one was open for 1% of the time, Pallas kernels for 0%

commit v1 on v0

v1 whole, which is shorter than its diff:
```python
import functools

import jax
import jax.numpy as jnp
from jax import lax
from jax.experimental import pallas as pl
from jax.experimental.pallas import tpu as pltpu
from jax.sharding import PartitionSpec as P

LAG = 64

contact_radius = 1.2
contact_width = 0.25
LANES = 128
SUB = 8
MESH = pl.DeviceIdType.MESH


def features_kernel(atoms, coords_ref, ia_ref, ib_ref, out_ref, a_pos, b_pos):
    per_frame = 3 * atoms
    res = coords_ref.shape[1]
    frames = coords_ref.shape[0] // per_frame
    nb = ib_ref.shape[1]
    na = out_ref.shape[1] // nb
    scale = 0.5 / contact_width

    def pick(ids):
        hot = lax.broadcasted_iota(jnp.int32, (res, ids.shape[1]), 0) == ids
        return jnp.dot(
            coords_ref[...], hot.astype(jnp.float32),
            precision=lax.Precision.HIGHEST, preferred_element_type=jnp.float32,
        ) * scale

    a_pos[...] = pick(ia_ref[...])
    b_pos[...] = pick(ib_ref[...])

    def frame_tile(tile, _):
        base = tile * (SUB * per_frame)

        def spread(a, _):
            where = jnp.full((SUB, LANES), a, jnp.int32)
            total = jnp.zeros((SUB, nb), jnp.float32)
            for p in range(atoms):
                left = [
                    jnp.take_along_axis(
                        a_pos[pl.ds(base + c * atoms + p, SUB, stride=per_frame), :], where, axis=1
                    )
                    for c in range(3)
                ]
                part = None
                for q in range(atoms):
                    square = None
                    for c in range(3):
                        d = left[c] - b_pos[pl.ds(base + c * atoms + q, SUB, stride=per_frame), :]
                        square = d * d if square is None else square + d * d
                    square = jnp.maximum(square, 1e-30)
                    half = jnp.tanh(scale * contact_radius - square * lax.rsqrt(square))
                    part = half if part is None else part + half
                total = total + (part + float(atoms))
            out_ref[pl.ds(pl.multiple_of(tile * SUB, SUB), SUB), pl.ds(pl.multiple_of(a * nb, LANES), nb)] = (
                total * (0.5 / atoms)
            )
            return 0

        lax.fori_loop(0, na, spread, 0)
        return 0

    lax.fori_loop(0, frames // SUB, frame_tile, 0)


def features(coords, index_a, set_b):
    frames, comps, atoms, res = coords.shape
    na, nb = index_a.shape[0], set_b.shape[0]
    ia = jnp.pad(index_a, (0, LANES - na)).reshape(1, LANES)
    vm = pl.BlockSpec(memory_space=pltpu.VMEM)
    return pl.pallas_call(
        functools.partial(features_kernel, atoms),
        out_shape=jax.ShapeDtypeStruct((frames, na * nb), jnp.float32),
        in_specs=[vm, vm, vm],
        out_specs=vm,
        scratch_shapes=[
            pltpu.VMEM((frames * comps * atoms, LANES), jnp.float32),
            pltpu.VMEM((frames * comps * atoms, nb), jnp.float32),
        ],
        compiler_params=pltpu.CompilerParams(vmem_limit_bytes=32 * 2**20),
    )(coords.reshape(frames * comps * atoms, res), ia, set_b.reshape(1, nb))


def gather_kernel(T, F, lifted_ref, rows_ref, cols_ref, sums, recv_rows, recv_cols, send_up, send_down,
                  send_x, send_cols, local_sem, sum_send, sum_recv):
    t = lax.axis_index("tm")
    f = lax.axis_index("feat")
    fr = lifted_ref.shape[0]
    width = cols_ref.shape[1]
    pairs = fr * T - LAG

    barrier = pltpu.get_barrier_semaphore()
    for k in range(1, T):
        pl.semaphore_signal(barrier, inc=1, device_id=(lax.rem(t + k, T), f), device_id_type=MESH)
    for k in range(1, F):
        pl.semaphore_signal(barrier, inc=1, device_id=(t, lax.rem(f + k, F)), device_id_type=MESH)

    ids = t * fr + lax.broadcasted_iota(jnp.int32, (fr, 1), 0)
    weight = (ids < pairs).astype(jnp.float32) + (ids >= LAG).astype(jnp.float32)
    sums[t] = jnp.sum(lifted_ref[...] * weight, axis=0, keepdims=True)
    pl.semaphore_wait(barrier, T - 1 + F - 1)

    def sum_copy(k):
        return pltpu.make_async_remote_copy(
            src_ref=sums.at[t], dst_ref=sums.at[t], send_sem=sum_send.at[k], recv_sem=sum_recv.at[t],
            device_id=(lax.rem(t + k, T), f), device_id_type=MESH,
        )

    for k in range(1, T):
        sum_copy(k).start()
    for k in range(1, T):
        other = lax.rem(t + k, T)
        pltpu.make_async_remote_copy(
            src_ref=sums.at[other], dst_ref=sums.at[other], send_sem=sum_send.at[k], recv_sem=sum_recv.at[other],
            device_id=(other, f), device_id_type=MESH,
        ).wait_recv()
    total = sums[0]
    for k in range(1, T):
        total = total + sums[k]
    means = total / (2.0 * pairs)
    rows_ref[pl.ds(pl.multiple_of(t * fr, fr), fr), :] = (lifted_ref[...] - means).astype(jnp.bfloat16)

    m = T // 2
    o = t // 2
    i = t % 2
    owner = t * F // T
    off = pl.multiple_of((t % (T // F)) * width, LANES)
    bits = [1 << b for b in range(F.bit_length() - 1)][::-1]
    r = 0
    for b in bits:
        r = r + b * ((f // b + owner // b) % 2)
    done = []

    def span(block):
        return pl.ds(pl.multiple_of(block * fr, fr), fr)

    def row_copy(block, target, sem):
        return pltpu.make_async_remote_copy(
            src_ref=rows_ref.at[span(block), :], dst_ref=rows_ref.at[span(block), :],
            send_sem=sem.at[block], recv_sem=recv_rows.at[block],
            device_id=(target, f), device_id_type=MESH,
        )

    def col_copy(block, bit, n, from_rows):
        src = rows_ref.at[span(block), pl.ds(off, width)] if from_rows else cols_ref.at[span(block), :]
        peer = f + bit - 2 * bit * ((f // bit) % 2)
        return pltpu.make_async_remote_copy(
            src_ref=src, dst_ref=cols_ref.at[span(block), :],
            send_sem=send_cols.at[n, block], recv_sem=recv_cols.at[block],
            device_id=(t, peer), device_id_type=MESH,
        )

    def local_copy(block):
        return pltpu.make_async_copy(
            rows_ref.at[span(block), pl.ds(off, width)], cols_ref.at[span(block), :], local_sem.at[block]
        )

    def fire(cond, make, wait="send"):
        @pl.when(cond)
        def _():
            make().start()

        done.append((cond, make, wait))

    def cols_from_rows(valid, block):
        for n, bit in enumerate(bits):
            fire(valid & (r == 0), functools.partial(col_copy, block, bit, n, True))
        fire(valid & (r == 0), functools.partial(local_copy, block), "all")

    def cols_onward(valid, block):
        @pl.when(valid & (r != 0))
        def _():
            col_copy(block, bits[0], 0, False).wait_recv()

        for n, bit in enumerate(bits[1:], 1):
            fire(valid & (r != 0) & (r % (2 * bit) == 0), functools.partial(col_copy, block, bit, n, False))

    def at_step(s, lane):
        if s < 0 or s >= m:
            return []
        found = [(o - s >= 0, (o - s) * 2 + lane, True)]
        if s > 0:
            found.append((o + s < m, (o + s) * 2 + lane, False))
        return found

    yes = t >= 0
    for s in range(m + 3):
        for valid, block, below in at_step(s, i):
            if s > 0:
                @pl.when(valid)
                def _():
                    row_copy(block, t, send_x).wait_recv()
            if below or s == 0:
                fire(valid & (o + 1 < m), functools.partial(row_copy, block, t + 2, send_up))
            if not below or s == 0:
                fire(valid & (o >= 1), functools.partial(row_copy, block, t - 2, send_down))
            fire(valid, functools.partial(row_copy, block, o * 2 + 1 - i, send_x))
            cols_from_rows(valid, block)
        for valid, block, below in at_step(s - 1, 1 - i):
            @pl.when(valid)
            def _():
                row_copy(block, t, send_x).wait_recv()

            cols_from_rows(valid, block)
        for valid, block, below in at_step(s - 2, i) + at_step(s - 3, 1 - i):
            cols_onward(valid, block)
    for k in range(1, T):
        sum_copy(k).wait_send()
    for cond, make, wait in done:
        @pl.when(cond)
        def _():
            if wait == "send":
                make().wait_send()
            else:
                make().wait()


def gather(lifted, T, F):
    fr, feats = lifted.shape
    width = feats * F // T
    vm = pl.BlockSpec(memory_space=pltpu.VMEM)
    dma = pltpu.SemaphoreType.DMA
    return pl.pallas_call(
        functools.partial(gather_kernel, T, F),
        out_shape=(
            jax.ShapeDtypeStruct((fr * T, feats), jnp.bfloat16),
            jax.ShapeDtypeStruct((fr * T, width), jnp.bfloat16),
        ),
        in_specs=[vm],
        out_specs=(vm, vm),
        scratch_shapes=[
            pltpu.VMEM((T, 1, feats), jnp.float32),
            dma((T,)), dma((T,)), dma((T,)), dma((T,)), dma((T,)), dma((F, T)), dma((T,)), dma((T,)), dma((T,)),
        ],
        compiler_params=pltpu.CompilerParams(
            collective_id=0, has_side_effects=True, vmem_limit_bytes=48 * 2**20
        ),
    )(lifted)


def product_kernel(pairs, rows_ref, cols_ref, c00_ref, c0t_ref, plus_cols, minus_cols, plus_t, minus_t):
    def halves(ref, at):
        early = ref[:pairs, at].astype(jnp.float32)
        later = ref[LAG:, at].astype(jnp.float32)
        return (early + later).astype(jnp.bfloat16), (early - later).astype(jnp.bfloat16)

    width = cols_ref.shape[1]
    step = min(width, 512)

    @pl.when(pl.program_id(0) == 0)
    def _():
        for at in range(0, width, step):
            plus_cols[:, at:at + step], minus_cols[:, at:at + step] = halves(cols_ref, slice(at, at + step))

    plus_rows, minus_rows = halves(rows_ref, slice(None))
    plus_t[...] = plus_rows.T
    minus_t[...] = minus_rows.T
    share = 1.0 / (4.0 * pairs)

    def columns(n, _):
        at = pl.ds(pl.multiple_of(n * step, step), step)
        sum_plus = jnp.dot(plus_t[...], plus_cols[:, at], preferred_element_type=jnp.float32)
        sum_minus = jnp.dot(minus_t[...], minus_cols[:, at], preferred_element_type=jnp.float32)
        c00_ref[:, at] = (sum_plus + sum_minus) * share
        c0t_ref[:, at] = (sum_plus - sum_minus) * share
        return 0

    lax.fori_loop(0, width // step, columns, 0)


def products(rows, cols):
    frames, height = rows.shape
    width = cols.shape[1]
    pairs = frames - LAG
    tile = 512 if frames <= 1024 else 256
    out = jax.ShapeDtypeStruct((height, width), jnp.float32)
    spec = pl.BlockSpec((tile, width), lambda n: (n, 0))
    return pl.pallas_call(
        functools.partial(product_kernel, pairs),
        out_shape=(out, out),
        grid=(height // tile,),
        in_specs=[pl.BlockSpec((frames, tile), lambda n: (0, n)), pl.BlockSpec((frames, width), lambda n: (0, 0))],
        out_specs=(spec, spec),
        scratch_shapes=[pltpu.VMEM((pairs, width), jnp.bfloat16)] * 2 + [pltpu.VMEM((tile, pairs), jnp.bfloat16)] * 2,
        compiler_params=pltpu.CompilerParams(vmem_limit_bytes=56 * 2**20),
    )(rows, cols)


def solution(mesh):
    T, F = mesh.shape["tm"], mesh.shape["feat"]

    def per_device(coords, set_a, set_b):
        rows_a = set_a.shape[0] // F
        index_a = lax.dynamic_slice_in_dim(set_a, lax.axis_index("feat") * rows_a, rows_a)
        lifted = features(coords, index_a, set_b)
        rows, cols = gather(lifted, T, F)
        return products(rows, cols)

    return jax.shard_map(
        per_device,
        mesh=mesh,
        in_specs=(P("tm", None, None, None), P(), P()),
        out_specs=(P("feat", "tm"), P("feat", "tm")),
        check_vma=False,
    )
```

time: 303 us -> 157 us (0.52)
  Pallas kernels: 0 us -> 150 us
  blocking collectives: 113 us -> 0 us
  other arithmetic: 65.3 us -> 0 us
  matrix products: 52.1 us -> 0 us
  waiting for transfers between devices: 46.4 us -> 0 us
  between operations: 14.2 us -> 0.66 us
  local copies, waits for them, and re-layouts: 9.68 us -> 4.1 us
    pallas_call x0 -> x3, Pallas kernels: none -> 150 us  [the longest x1 63.5 us: gather(): pl.pallas_call(functools.partial(gather_kernel, T, F), out_shape=(jax.Sha...]
    all_to_all x1 -> x0, blocking collectives: 86.8 us -> none  [per_device(): lax.all_to_all(every_feature, 'tm', split_axis=1, concat_axis=0, tiled=True)]
    dot_general x3 -> x0, matrix products: 52.1 us -> none  [the longest x2 51 us: contract_frames(): lax.dot_general(left, right, (((0,), (0,)), ((), ())), preferred_element_...]
    reduce_sum x2 -> x0, other arithmetic: 51.5 us -> none  [contact_features(): jnp.sum(jax.nn.sigmoid((contact_radius - jnp.sqrt(square)) / contact_widt...]
    all_gather x2 -> x0, waiting for transfers between devices: 45.7 us -> none  [the longest x1 29.9 us: per_device(): every_feature = lax.all_gather(centered, 'feat', axis=1, tiled=True)]
    psum x1 -> x0, blocking collectives: 26.1 us -> none  [per_device(): means = lax.psum(local_sums, 'tm') / (2.0 * pairs)]
    convert_element_type x3 -> x0, other arithmetic: 9 us -> none  [the longest x2 7.62 us: pair_sums(): (early - later).astype(jnp.bfloat16)]
  transfers between devices with their start and end apart: 2 -> 0, of which waited for: 2 -> 0; matrix products, arithmetic and copies ran while one was open for 1% -> 0% of each run, Pallas kernels for 0% -> 0%
where the time goes in v1:
time: 157 us; the launch traced here: 155 us
  Pallas kernels  150 us (96%)
  local copies, waits for them, and re-layouts  4.1 us (3%)
    pallas_call x1, Pallas kernels, gather(): pl.pallas_call(functools.partial(gather_kernel, T, F), out_shape=(jax.Sha...  63.5 us
    pallas_call x1, Pallas kernels, features(): pl.pallas_call(functools.partial(features_kernel, atoms), out_shape=jax.S...  54.5 us
    pallas_call x1, Pallas kernels, products(): pl.pallas_call(functools.partial(product_kernel, pairs), out_shape=(out,...  32.4 us
    unnamed x6, local copies, waits for them, and re-layouts  3.37 us

profile of v1, /device:TPU:7, one launch (start us, length us, event | category | flops | bytes accessed | tf_op | source)
XLA Modules:
  0.0 155.2 jit_solution(4610136091696393915)
XLA Ops:
  0.6 0.7 dynamic_slice.3
  1.4 0.0 copy-start.1
  1.4 1.4 copy-done.1
  2.8 0.0 copy-start.2
  2.8 0.7 copy-done.2
  3.4 54.5 %shard_map.50.lifted_ref = f32[64,4096]{1,0:T(8,128)S(1)} custom-call(f32[1536,256]{1,0:T(8,128)S(1)} %bitcast.4, s32[1,128]{1,0:T(1,128)S(1)} %pad_bitcast_fusion.ia_ref, s32[1,128]{1,0:T(1,128)S(1)} %bitcast.5), custom_call_target="tpu_custom_call" | custom-call | tf_op jit(solution)/shard_map/pallas_call | solution.py:76
  57.9 63.5 %shard_map.51 = (bf16[512,4096]{1,0:T(8,128)(2,1)}, bf16[512,2048]{1,0:T(8,128)(2,1)S(1)}) custom-call(f32[64,4096]{1,0:T(8,128)S(1)} %shard_map.50.lifted_ref), custom_call_target="tpu_custom_call" | custom-call | tf_op jit(solution)/shard_map/pallas_call | solution.py:228
  121.5 0.0 copy-start
  121.5 1.3 copy-done
  122.8 32.4 %shard_map.52 = (f32[4096,2048]{1,0:T(8,128)}, f32[4096,2048]{1,0:T(8,128)}) custom-call(bf16[512,4096]{1,0:T(8,128)(2,1)} %get-tuple-element.4.rows_ref, bf16[512,2048]{1,0:T(8,128)(2,1)} %copy-done), custom_call_target="tpu_custom_call" | custom-call | tf_op jit(solution)/shard_map/pallas_call | solution.py:283
  (1 shorter events, 0.0 us)
Async XLA Ops:
  1.4 1.4 copy-start.1
  2.8 0.7 copy-start.2
  121.5 1.3 copy-start

commit v2 on v1

v2 whole, which is shorter than its diff:
```python
import functools

import jax
import jax.numpy as jnp
from jax import lax
from jax.experimental import pallas as pl
from jax.experimental.pallas import tpu as pltpu
from jax.sharding import PartitionSpec as P

LAG = 64

contact_radius = 1.2
contact_width = 0.25
LANES = 128
SUB = 8
CHUNKS = 4
MESH = pl.DeviceIdType.MESH


def pick_kernel(coords_ref, ia_ref, ib_ref, a_ref, b_ref, a_all, b_all):
    tiles, per_frame = a_ref.shape[:2]
    res = coords_ref.shape[1]
    scale = 0.5 / contact_width
    hot = jnp.concatenate(
        [
            (lax.broadcasted_iota(jnp.int32, (res, LANES), 0) == ref[...]).astype(jnp.bfloat16)
            for ref in (ia_ref, ib_ref)
        ],
        axis=1,
    )

    def one(tile, _):
        count = SUB * per_frame
        x = coords_ref[pl.ds(pl.multiple_of(tile * count, SUB), count), :]
        high = x.astype(jnp.bfloat16)
        rest = x - high.astype(jnp.float32)
        middle = rest.astype(jnp.bfloat16)
        low = (rest - middle.astype(jnp.float32)).astype(jnp.bfloat16)
        got = jnp.dot(low, hot, preferred_element_type=jnp.float32)
        got = got + jnp.dot(middle, hot, preferred_element_type=jnp.float32)
        got = (got + jnp.dot(high, hot, preferred_element_type=jnp.float32)) * scale
        a_all[...] = got[:, :LANES]
        b_all[...] = got[:, LANES:]
        for k in range(per_frame):
            a_ref[tile, k] = a_all[pl.ds(k, SUB, stride=per_frame), :]
            b_ref[tile, k] = b_all[pl.ds(k, SUB, stride=per_frame), :]
        return 0

    lax.fori_loop(0, tiles, one, 0)


def pick(coords, index_a, set_b):
    frames, comps, atoms, res = coords.shape
    na, nb = index_a.shape[0], set_b.shape[0]
    ia = jnp.pad(index_a, (0, LANES - na)).reshape(1, LANES)
    vm = pl.BlockSpec(memory_space=pltpu.VMEM)
    out = jax.ShapeDtypeStruct((frames // SUB, comps * atoms, SUB, LANES), jnp.float32)
    return pl.pallas_call(
        pick_kernel,
        out_shape=(out, out),
        in_specs=[vm, vm, vm],
        out_specs=(vm, vm),
        scratch_shapes=[pltpu.VMEM((SUB * comps * atoms, LANES), jnp.float32)] * 2,
        compiler_params=pltpu.CompilerParams(vmem_limit_bytes=16 * 2**20),
    )(coords.reshape(frames * comps * atoms, res), ia, set_b.reshape(1, nb))


def gather_kernel(T, F, chunks, a_ref, b_ref, rows_ref, cols_ref, lifted_ref, spread, sums, recv_rows,
                  recv_cols, send_up, send_down, send_x, send_cols, local_sem, sum_send, sum_recv):
    t = lax.axis_index("tm")
    f = lax.axis_index("feat")
    tiles, per_frame = a_ref.shape[:2]
    atoms = per_frame // 3
    fr, feats = lifted_ref.shape
    wide = feats // chunks
    each = wide // LANES
    width = cols_ref.shape[1]
    pairs = fr * T - LAG
    top = contact_radius * 0.5 / contact_width

    barrier = pltpu.get_barrier_semaphore()
    for k in range(1, T):
        pl.semaphore_signal(barrier, inc=1, device_id=(lax.rem(t + k, T), f), device_id_type=MESH)
    for k in range(1, F):
        pl.semaphore_signal(barrier, inc=1, device_id=(t, lax.rem(f + k, F)), device_id_type=MESH)

    def compute(c, first, count):
        def prepare(n, side):
            tile = first + n // each
            where = jnp.full((per_frame * SUB, LANES), c * each + n % each, jnp.int32)
            got = jnp.take_along_axis(a_ref[tile].reshape(per_frame * SUB, LANES), where, axis=1)
            spread[side] = got.reshape(per_frame, SUB, LANES)

        prepare(0, 0)
        last = count * each - 1

        def one(n, _):
            tile = first + n // each
            prepare(jnp.minimum(n + 1, last), (n + 1) % 2)
            total = None
            for p in range(atoms):
                square = None
                for k in range(3):
                    d = spread[n % 2, k * atoms + p][None] - b_ref[tile, k * atoms:(k + 1) * atoms]
                    square = d * d if square is None else square + d * d
                square = jnp.maximum(square, 1e-30)
                half = jnp.sum(jnp.tanh(top - square * lax.rsqrt(square)), axis=0) + float(atoms)
                total = half if total is None else total + half
            lifted_ref[
                pl.ds(pl.multiple_of(tile * SUB, SUB), SUB),
                pl.ds(pl.multiple_of(c * wide + (n % each) * LANES, LANES), LANES),
            ] = total * (0.5 / atoms)
            return 0

        lax.fori_loop(0, last + 1, one, 0)

    def sum_copy(c, source, k):
        return pltpu.make_async_remote_copy(
            src_ref=sums.at[c, source], dst_ref=sums.at[c, source],
            send_sem=sum_send.at[c, k], recv_sem=sum_recv.at[c, source],
            device_id=(lax.rem(t + k, T), f), device_id_type=MESH,
        )

    def send_sums(c):
        ids = t * fr + lax.broadcasted_iota(jnp.int32, (fr, 1), 0)
        weight = (ids < pairs).astype(jnp.float32) + (ids >= LAG).astype(jnp.float32)
        sums[c, t] = jnp.sum(lifted_ref[:, c * wide:(c + 1) * wide] * weight, axis=0, keepdims=True)
        if c == 0:
            pl.semaphore_wait(barrier, T - 1 + F - 1)
        for k in range(1, T):
            sum_copy(c, t, k).start()

    def center(c):
        for k in range(1, T):
            sum_copy(c, lax.rem(t + k, T), k).wait_recv()
        total = sums[c, 0]
        for k in range(1, T):
            total = total + sums[c, k]
        means = total / (2.0 * pairs)
        at = slice(c * wide, (c + 1) * wide)
        rows_ref[pl.ds(pl.multiple_of(t * fr, fr), fr), at] = (lifted_ref[:, at] - means).astype(jnp.bfloat16)

    m = T // 2
    o = t // 2
    i = t % 2
    owner = t * F // T
    part = t % (T // F)
    bits = [1 << b for b in range(F.bit_length() - 1)][::-1]
    r = 0
    for b in bits:
        r = r + b * ((f // b + owner // b) % 2)
    done = []

    def span(block):
        return pl.ds(pl.multiple_of(block * fr, fr), fr)

    piece = min(wide, width)
    per_chunk = wide // piece

    def row_copy(c, block, target, sem):
        at = rows_ref.at[span(block), pl.ds(c * wide, wide)]
        return pltpu.make_async_remote_copy(
            src_ref=at, dst_ref=at, send_sem=sem.at[c, block], recv_sem=recv_rows.at[c, block],
            device_id=(target, f), device_id_type=MESH,
        )

    def in_rows(g, block):
        return rows_ref.at[span(block), pl.ds(g * piece, piece)]

    def in_cols(g, block):
        return cols_ref.at[span(block), pl.ds(g * piece % width, piece)]

    def col_copy(g, block, bit, n, from_rows):
        peer = f + bit - 2 * bit * ((f // bit) % 2)
        return pltpu.make_async_remote_copy(
            src_ref=in_rows(g, block) if from_rows else in_cols(g, block), dst_ref=in_cols(g, block),
            send_sem=send_cols.at[n, g, block], recv_sem=recv_cols.at[g, block],
            device_id=(t, peer), device_id_type=MESH,
        )

    def local_copy(g, block):
        return pltpu.make_async_copy(in_rows(g, block), in_cols(g, block), local_sem.at[g, block])

    def fire(cond, make, wait="send"):
        @pl.when(cond)
        def _():
            make().start()

        done.append((cond, make, wait))

    def blocks_of(c):
        for g in range(c * per_chunk, (c + 1) * per_chunk):
            yield g, part == g * piece // width

    def cols_from_rows(c, valid, block):
        for g, mine in blocks_of(c):
            for n, bit in enumerate(bits):
                fire(valid & mine & (r == 0), functools.partial(col_copy, g, block, bit, n, True))
            fire(valid & mine & (r == 0), functools.partial(local_copy, g, block), "all")

    def cols_onward(c, valid, block):
        for g, mine in blocks_of(c):
            here = valid & mine & (r != 0)

            @pl.when(here)
            def _():
                col_copy(g, block, bits[0], 0, False).wait_recv()

            for n, bit in enumerate(bits[1:], 1):
                fire(here & (r % (2 * bit) == 0), functools.partial(col_copy, g, block, bit, n, False))

    def at_step(s, lane):
        if s < 0 or s >= m:
            return []
        found = [(o - s >= 0, (o - s) * 2 + lane, True)]
        if s > 0:
            found.append((o + s < m, (o + s) * 2 + lane, False))
        return found

    def step(c, s):
        if s == 0:
            center(c)
        for valid, block, below in at_step(s, i):
            if s > 0:
                @pl.when(valid)
                def _():
                    row_copy(c, block, t, send_x).wait_recv()
            if below or s == 0:
                fire(valid & (o + 1 < m), functools.partial(row_copy, c, block, t + 2, send_up))
            if not below or s == 0:
                fire(valid & (o >= 1), functools.partial(row_copy, c, block, t - 2, send_down))
            fire(valid, functools.partial(row_copy, c, block, o * 2 + 1 - i, send_x))
            cols_from_rows(c, valid, block)
        for valid, block, below in at_step(s - 1, 1 - i):
            @pl.when(valid)
            def _():
                row_copy(c, block, t, send_x).wait_recv()

            cols_from_rows(c, valid, block)
        for valid, block, below in at_step(s - 2, i) + at_step(s - 3, 1 - i):
            cols_onward(c, valid, block)

    for slot in range(2 * chunks + m + 3):
        c, h = slot // 2, slot % 2
        if c < chunks:
            compute(c, h * (tiles // 2), tiles // 2)
            if h == 1:
                send_sums(c)
        for c in range(chunks):
            s = slot - 2 * c - 2
            if 0 <= s < m + 3:
                step(c, s)
    for c in range(chunks):
        for k in range(1, T):
            sum_copy(c, t, k).wait_send()
    for cond, make, wait in done:
        @pl.when(cond)
        def _():
            if wait == "send":
                make().wait_send()
            else:
                make().wait()


def gather(a_pos, b_pos, na, T, F):
    tiles, per_frame = a_pos.shape[:2]
    fr, feats = tiles * SUB, na * b_pos.shape[3]
    width = feats * F // T
    chunks = CHUNKS if T <= 8 else 4
    pieces = max(chunks, feats // width)
    vm = pl.BlockSpec(memory_space=pltpu.VMEM)
    dma = pltpu.SemaphoreType.DMA
    return pl.pallas_call(
        functools.partial(gather_kernel, T, F, chunks),
        out_shape=(
            jax.ShapeDtypeStruct((fr * T, feats), jnp.bfloat16),
            jax.ShapeDtypeStruct((fr * T, width), jnp.bfloat16),
        ),
        in_specs=[vm, vm],
        out_specs=(vm, vm),
        scratch_shapes=[
            pltpu.VMEM((fr, feats), jnp.float32),
            pltpu.VMEM((2, per_frame, SUB, LANES), jnp.float32),
            pltpu.VMEM((chunks, T, 1, feats // chunks), jnp.float32),
            dma((chunks, T)), dma((pieces, T)), dma((chunks, T)), dma((chunks, T)), dma((chunks, T)),
            dma((F.bit_length(), pieces, T)), dma((pieces, T)), dma((chunks, T)), dma((chunks, T)),
        ],
        compiler_params=pltpu.CompilerParams(
            collective_id=0, has_side_effects=True, vmem_limit_bytes=48 * 2**20
        ),
    )(a_pos, b_pos)


def product_kernel(pairs, rows_ref, cols_ref, c00_ref, c0t_ref, plus_cols, minus_cols, plus_t, minus_t):
    def halves(ref, at):
        early = ref[:pairs, at].astype(jnp.float32)
        later = ref[LAG:, at].astype(jnp.float32)
        return (early + later).astype(jnp.bfloat16), (early - later).astype(jnp.bfloat16)

    width = cols_ref.shape[1]
    step = min(width, 512)

    @pl.when(pl.program_id(0) == 0)
    def _():
        for at in range(0, width, step):
            plus_cols[:, at:at + step], minus_cols[:, at:at + step] = halves(cols_ref, slice(at, at + step))

    plus_rows, minus_rows = halves(rows_ref, slice(None))
    plus_t[...] = plus_rows.T
    minus_t[...] = minus_rows.T
    share = 1.0 / (4.0 * pairs)

    def columns(n, _):
        at = pl.ds(pl.multiple_of(n * step, step), step)
        sum_plus = jnp.dot(plus_t[...], plus_cols[:, at], preferred_element_type=jnp.float32)
        sum_minus = jnp.dot(minus_t[...], minus_cols[:, at], preferred_element_type=jnp.float32)
        c00_ref[:, at] = (sum_plus + sum_minus) * share
        c0t_ref[:, at] = (sum_plus - sum_minus) * share
        return 0

    lax.fori_loop(0, width // step, columns, 0)


def products(rows, cols):
    frames, height = rows.shape
    width = cols.shape[1]
    pairs = frames - LAG
    tile = 512 if frames <= 1024 else 256
    out = jax.ShapeDtypeStruct((height, width), jnp.float32)
    spec = pl.BlockSpec((tile, width), lambda n: (n, 0))
    return pl.pallas_call(
        functools.partial(product_kernel, pairs),
        out_shape=(out, out),
        grid=(height // tile,),
        in_specs=[pl.BlockSpec((frames, tile), lambda n: (0, n)), pl.BlockSpec((frames, width), lambda n: (0, 0))],
        out_specs=(spec, spec),
        scratch_shapes=[pltpu.VMEM((pairs, width), jnp.bfloat16)] * 2 + [pltpu.VMEM((tile, pairs), jnp.bfloat16)] * 2,
        compiler_params=pltpu.CompilerParams(vmem_limit_bytes=56 * 2**20),
    )(rows, cols)


def solution(mesh):
    T, F = mesh.shape["tm"], mesh.shape["feat"]

    def per_device(coords, set_a, set_b):
        rows_a = set_a.shape[0] // F
        index_a = lax.dynamic_slice_in_dim(set_a, lax.axis_index("feat") * rows_a, rows_a)
        a_pos, b_pos = pick(coords, index_a, set_b)
        rows, cols = gather(a_pos, b_pos, rows_a, T, F)
        return products(rows, cols)

    return jax.shard_map(
        per_device,
        mesh=mesh,
        in_specs=(P("tm", None, None, None), P(), P()),
        out_specs=(P("feat", "tm"), P("feat", "tm")),
        check_vma=False,
    )
```

time: 157 us -> 136 us (0.87); the launches traced: 155 us -> 136 us
  Pallas kernels: 150 us -> 131 us
    pallas_call x2, Pallas kernels: 118 us -> 98.7 us  [the longest x1 96.4 us: gather(): pl.pallas_call(functools.partial(gather_kernel, T, F, chunks), out_shape=...]
where the time goes in v2:
time: 136 us
  Pallas kernels  131 us (96%)
  local copies, waits for them, and re-layouts  4.12 us (3%)
    pallas_call x1, Pallas kernels, gather(): pl.pallas_call(functools.partial(gather_kernel, T, F, chunks), out_shape=...  96.4 us
    pallas_call x1, Pallas kernels, products(): pl.pallas_call(functools.partial(product_kernel, pairs), out_shape=(out,...  32.4 us
    unnamed x6, local copies, waits for them, and re-layouts  3.38 us

profile of v2, /device:TPU:7, one launch (start us, length us, event | category | flops | bytes accessed | tf_op | source)
XLA Modules:
  0.0 135.8 jit_solution(2940614523737619735)
XLA Ops:
  0.6 0.7 dynamic_slice.3
  1.4 0.0 copy-start.1
  1.4 1.4 %copy-done.1 = f32[64,3,8,256]{3,2,1,0:T(8,128)S(1)} copy-done((f32[64,3,8,256]{3,2,1,0:T(8,128)S(1)}, f32[64,3,8,256]{3,2,1,0:T(8,128)}, u32[]{:S(2)}) %copy-start.1) | copy-done | bytes 1572888
  2.8 0.0 copy-start.2
  2.8 0.7 copy-done.2
  3.4 2.3 %shard_map.50 = (f32[8,24,8,128]{3,2,1,0:T(8,128)S(1)}, f32[8,24,8,128]{3,2,1,0:T(8,128)S(1)}) custom-call(f32[1536,256]{1,0:T(8,128)S(1)} %bitcast.4, s32[1,128]{1,0:T(1,128)S(1)} %pad_bitcast_fusion.ia_ref, s32[1,128]{1,0:T(1,128)S(1)} %bitcast.5), custom_call_target="tpu_custom_call" | custom-call | tf_op jit(solution)/shard_map/pallas_call | solution.py:58
  5.7 96.4 %shard_map.51 = (bf16[512,4096]{1,0:T(8,128)(2,1)}, bf16[512,2048]{1,0:T(8,128)(2,1)S(1)}) custom-call(f32[8,24,8,128]{3,2,1,0:T(8,128)S(1)} %get-tuple-element.6.a_ref, f32[8,24,8,128]{3,2,1,0:T(8,128)S(1)} %get-tuple-element.7.b_ref), custom_call_target="tpu_custom_call" | custom-call | tf_op jit(solution)/shard_map/pallas_call | solution.py:273
  102.2 0.0 copy-start
  102.2 1.3 copy-done
  103.5 32.4 %shard_map.52 = (f32[4096,2048]{1,0:T(8,128)}, f32[4096,2048]{1,0:T(8,128)}) custom-call(bf16[512,4096]{1,0:T(8,128)(2,1)} %get-tuple-element.8.rows_ref, bf16[512,2048]{1,0:T(8,128)(2,1)} %copy-done), custom_call_target="tpu_custom_call" | custom-call | tf_op jit(solution)/shard_map/pallas_call | solution.py:331
  (1 shorter events, 0.0 us)
Async XLA Ops:
  1.4 1.4 %copy-start.1 = (f32[64,3,8,256]{3,2,1,0:T(8,128)S(1)}, f32[64,3,8,256]{3,2,1,0:T(8,128)}, u32[]{:S(2)}) copy-start(f32[64,3,8,256]{3,2,1,0:T(8,128)} %param.3) | copy-start | bytes 4718596
  2.8 0.7 copy-start.2
  102.2 1.3 copy-start
